TPU v7x, 256 devices: a whole 4x4x8 slice. The times are simulated.
256 devices in a mesh: gx: 32 (over z_hi, x, core), gy: 8 (over z_lo, y).
Axes of the slice: x: 4, y: 4, z: 8 (z_hi: 4, z_lo: 2; z = z_hi * 2 + z_lo), core: 2. Of those that a mesh axis runs over, the one named last changes fastest.
Arguments:
- checkpoint: float32 [19, 256, 2048], P(None, 'gx', 'gy'), as said below
- cotangent: float32 [19, 256, 2048], P(None, 'gx', 'gy'), may hold values from -6 to 6
- blade_area: float32 [1536], replicated, may hold values from 0.5 to 2
- hub_tile: int32 [16], replicated, may hold values from 0 to 255
- point_side: int32 [1536], replicated, may hold values from 0 to 8
- point_local: int32 [1536], replicated, may hold values from 0 to 2047
Outputs:
- grad_checkpoint: float32 [19, 256, 2048], P(None, 'gx', 'gy')
- grad_area: float32 [1536], replicated
Inputs may be any that keep to these rules, and one draw needn't show every extreme that they name: `hub_tile`: tile ids count every tile of the slab. `point_side`: every actuator point lies in its hub tile or one of the eight tiles around it. `checkpoint`: populations are positive and near a local equilibrium with density near one and streamwise velocity near 0.08.
All inputs are finite; a program needn't handle non-finite values.
Results may differ from a plain program's by a relative error of at most 0.0003.
Values sent between devices are 32-bit elements; how exact they have to be, the bound alone decides.
No kernel may reach another device: no remote copies, remote signals or barrier semaphores. Data moves between devices by JAX's collectives and lax.ppermute only.
A program may use at most 128 MiB of HBM per device.

v0:
```python
import jax
import jax.numpy as jnp
import numpy as np
from jax import lax
from jax.sharding import PartitionSpec as P

NZ = 16
STEPS = 4
NTURB = 16
PTS = 96
TAU_ZERO = 0.52
SMAGORINSKY = 0.17 * 0.17
TINY = 1e-10
THRUST = 4.0
GHOST_RATES = np.array([1.05, 1.15, 1.25, 1.35, 1.45, 1.55, 1.65, 1.75, 1.85])


def extended(value, sides, width):
    for axis, dim in sides:
        size, length = (lax.axis_size(axis), value.shape[dim])
        up = [(i, (i + 1) % size) for i in range(size)]
        down = [(j, i) for i, j in up]
        last = lax.slice_in_dim(value, length - width, length, axis=dim)
        first = lax.slice_in_dim(value, 0, width, axis=dim)
        before = lax.ppermute(last, axis, up)
        after = lax.ppermute(first, axis, down)
        value = jnp.concatenate([before, value, after], axis=dim)
    return value


def lattice():
    axis_part = [(1, 0, 0), (-1, 0, 0), (0, 1, 0), (0, -1, 0), (0, 0, 1), (0, 0, -1)]
    edge_part = [
        (1, 1, 0),
        (-1, -1, 0),
        (1, -1, 0),
        (-1, 1, 0),
        (1, 0, 1),
        (-1, 0, -1),
        (1, 0, -1),
        (-1, 0, 1),
        (0, 1, 1),
        (0, -1, -1),
        (0, 1, -1),
        (0, -1, 1),
    ]
    vectors = np.array([(0, 0, 0)] + axis_part + edge_part) * 1.0
    weights = np.array([1.0 / 3.0] + [1.0 / 18.0] * 6 + [1.0 / 36.0] * 12)
    opposite = np.array(
        [int(np.argmin(np.abs(vectors + vectors[column]).sum(1))) for column in range(19)]
    )
    return (vectors, weights, opposite)


def orthonormal(monomials, weights):
    rows = []
    for entry in monomials:
        vector = entry * 1.0
        for sweep in range(2):
            for other in rows:
                vector = vector - np.sum(weights * vector * other) * other
        vector = vector / np.sqrt(np.sum(weights * vector * vector))
        rows.append(vector)
    return np.stack(rows, 0)


def tables():
    vectors, weights, opposite = lattice()
    along_x, along_y, along_z = (vectors[:, 0], vectors[:, 1], vectors[:, 2])
    monomials = [
        np.ones(19),
        along_x,
        along_y,
        along_z,
        along_x * along_x,
        along_y * along_y,
        along_z * along_z,
        along_x * along_y,
        along_x * along_z,
        along_y * along_z,
        along_x * along_y * along_y,
        along_x * along_z * along_z,
        along_y * along_x * along_x,
        along_y * along_z * along_z,
        along_z * along_x * along_x,
        along_z * along_y * along_y,
        along_x * along_x * along_y * along_y,
        along_x * along_x * along_z * along_z,
        along_y * along_y * along_z * along_z,
    ]
    basis = orthonormal(monomials, weights)
    second = weights[:, None] * basis[4:10].T
    ghost = weights[:, None] * basis[10:].T * GHOST_RATES[None, :]
    stress = np.stack(
        [
            along_x * along_x,
            along_y * along_y,
            along_z * along_z,
            along_x * along_y,
            along_x * along_z,
            along_y * along_z,
        ],
        0,
    )
    push = 3.0 * weights * along_x
    return {
        "vectors": vectors,
        "weights": weights,
        "opposite": opposite,
        "high": jnp.asarray(basis[4:], jnp.float32),
        "second": jnp.asarray(second, jnp.float32),
        "ghost": jnp.asarray(ghost, jnp.float32),
        "stress": jnp.asarray(stress, jnp.float32),
        "push": jnp.asarray(push, jnp.float32),
        "velt": jnp.asarray(vectors.T, jnp.float32),
        "wvec": jnp.asarray(weights, jnp.float32),
        "vecs": jnp.asarray(vectors, jnp.float32),
    }


def streamwise_velocity(flat, table):
    density = jnp.sum(flat, 0)
    momentum = jnp.dot(table["velt"], flat, precision=lax.Precision.HIGHEST)
    return momentum[0] / density


def collide(flat, force, table):
    density = jnp.sum(flat, 0)
    momentum = jnp.dot(table["velt"], flat, precision=lax.Precision.HIGHEST)
    velocity = momentum / density[None, :]
    project = jnp.dot(table["vecs"], velocity, precision=lax.Precision.HIGHEST)
    speed_sq = jnp.sum(velocity * velocity, 0)
    equil = (
        table["wvec"][:, None]
        * density[None, :]
        * (1.0 + 3.0 * project + 4.5 * project * project - 1.5 * speed_sq[None, :])
    )
    noneq = flat - equil
    stress = jnp.dot(table["stress"], noneq, precision=lax.Precision.HIGHEST)
    square = jnp.sum(stress[:3] * stress[:3], 0) + 2.0 * jnp.sum(stress[3:] * stress[3:], 0)
    relax_time = 0.5 * (
        TAU_ZERO
        + jnp.sqrt(TAU_ZERO * TAU_ZERO + 18.0 * SMAGORINSKY * jnp.sqrt(square + TINY) / density)
    )
    moments = jnp.dot(table["high"], noneq, precision=lax.Precision.HIGHEST)
    relaxed = jnp.dot(
        table["second"], moments[:6] / relax_time[None, :], precision=lax.Precision.HIGHEST
    )
    relaxed = relaxed + jnp.dot(table["ghost"], moments[6:], precision=lax.Precision.HIGHEST)
    return flat - relaxed + table["push"][:, None] * force[None, :]


def wall_mask(vectors, depth):
    keep = np.ones((19, depth))
    for column in range(19):
        if vectors[column, 2] > 0.5:
            keep[column, 0] = 0.0
        if vectors[column, 2] < -0.5:
            keep[column, depth - 1] = 0.0
    return keep


def neighbours(field, vectors, direction):
    pops, width_x, span = field.shape
    depth = NZ
    width_y = span // depth
    step_x = [int(direction * vectors[column, 0]) for column in range(19)]
    step_y = [int(direction * vectors[column, 1]) for column in range(19)]
    step_z = [int(direction * vectors[column, 2]) for column in range(19)]
    padded = extended(field.reshape(pops, width_x, width_y, depth), (("gx", 1), ("gy", 2)), 1)
    padded = padded.reshape(pops, width_x + 2, (width_y + 2) * depth)
    padded = jnp.pad(padded, ((0, 0), (0, 0), (1, 1)))
    pieces = []
    for column in range(19):
        start_x = 1 - step_x[column]
        start_j = depth + 1 - step_y[column] * depth - step_z[column]
        pieces.append(padded[column, start_x : start_x + width_x, start_j : start_j + span])
    return jnp.stack(pieces, 0)


def turbine_total(partial_value):
    return lax.psum(partial_value, ("gx", "gy"))


def body(checkpoint, cotangent, blade_area, hub_tile, point_side, point_local):
    table = tables()
    vectors = table["vectors"]
    opposite = table["opposite"]
    pops, width_x, span = checkpoint.shape
    width_y = span // NZ
    cells = width_x * span
    keep = jnp.asarray(np.tile(wall_mask(vectors, NZ), (1, width_y)), jnp.float32)[:, None, :]
    count_x = lax.axis_size("gx")
    count_y = lax.axis_size("gy")
    index_x = lax.axis_index("gx")
    index_y = lax.axis_index("gy")
    turbine = jnp.arange(NTURB * PTS, dtype=jnp.int32) // PTS
    hub_x = hub_tile // count_y
    hub_y = hub_tile % count_y
    tile_x = (hub_x[turbine] + point_side // 3 - 1) % count_x
    tile_y = (hub_y[turbine] + point_side % 3 - 1) % count_y
    mine = ((tile_x == index_x) & (tile_y == index_y)).astype(jnp.float32)
    denom = jnp.sum(blade_area.reshape(NTURB, PTS), 1)

    def stream_adjoint(adjoint):
        pushed = neighbours(adjoint * keep, vectors, -1)
        return pushed + ((1.0 - keep) * adjoint)[opposite]

    def collide_local(flat, force):
        return collide(flat, force, table)

    def velocity_local(flat):
        return streamwise_velocity(flat, table)

    field = checkpoint
    saved = []
    for counter in range(STEPS):
        flat = (neighbours(field, vectors, 1) * keep + (1.0 - keep) * field[opposite]).reshape(
            pops, cells
        )
        sampled = velocity_local(flat)[point_local] * mine
        numer = turbine_total(jnp.sum((blade_area * sampled).reshape(NTURB, PTS), 1))
        rotor = numer / denom
        thrust = -THRUST * blade_area * rotor[turbine] * sampled
        force = jnp.zeros((cells,), jnp.float32).at[point_local].add(thrust)
        saved.append((flat, sampled, rotor, force))
        field = collide_local(flat, force).reshape(pops, width_x, span)
    adjoint = cotangent
    area_grad = jnp.zeros_like(blade_area)
    for counter in range(STEPS - 1, -1, -1):
        flat, sampled, rotor, force = saved[counter]
        unused, pullback = jax.vjp(collide_local, flat, force)
        flat_bar, force_bar = pullback(adjoint.reshape(pops, cells))
        thrust_bar = force_bar[point_local] * mine
        rotor_here = rotor[turbine]
        sample_bar = thrust_bar * -THRUST * blade_area * rotor_here
        rotor_part = jnp.sum((thrust_bar * -THRUST * blade_area * sampled).reshape(NTURB, PTS), 1)
        rotor_bar = turbine_total(rotor_part)
        numer_bar = rotor_bar / denom
        sample_bar = sample_bar + numer_bar[turbine] * blade_area * mine
        area_grad = area_grad + thrust_bar * -THRUST * rotor_here * sampled
        area_grad = area_grad + mine * rotor_bar[turbine] * (sampled - rotor_here) / denom[turbine]
        speed_bar = jnp.zeros((cells,), jnp.float32).at[point_local].add(sample_bar)
        unused_speed, speed_pull = jax.vjp(velocity_local, flat)
        flat_bar = flat_bar + speed_pull(speed_bar)[0]
        adjoint = stream_adjoint(flat_bar.reshape(pops, width_x, span))
    grad_area = lax.psum(area_grad, ("gx", "gy"))
    return (adjoint, grad_area)


def solution(mesh):
    return jax.shard_map(
        body,
        mesh=mesh,
        in_specs=(P(None, "gx", "gy"), P(None, "gx", "gy"), P(), P(), P(), P()),
        out_specs=(P(None, "gx", "gy"), P()),
        check_vma=False,
    )
```

profile of v0, /device:TPU:1, one launch (start us, length us, event | category | flops | bytes accessed | tf_op | source)
XLA Modules:
  0.0 1147.3 jit_solution(11894280306716798596)
XLA Ops:
  2.0 2.7 collective-permute-start
  7.4 8.9 select_reduce_fusion.13
  18.5 3.0 collective-permute-start.3
  29.9 8.4 gather_fusion.1
  38.4 11.2 fusion.199
  49.9 82.5 %psum.63 = f32[16]{0:T(128)S(1)} all-reduce(f32[16]{0:T(128)S(1)} %reduce_sum.414), channel_id=1, replica_groups=mesh['gx'=32,'gy'=8] {'gx','gy'}, use_global_device_ids=true, to_apply=%region_5.6 | all-reduce | flops 16 | bytes 128 | tf_op jit(solution)/shard_map/psum | solution.py:182
  133.1 4.4 select_reduce_fusion.12
  137.6 5.7 multiply_multiply_fusion.26
  143.3 8.7 scatter_custom_fusion
  156.2 2.4 collective-permute-done.5
  159.3 3.2 collective-permute-start.7
  172.3 8.4 gather_fusion.3
  181.3 84.2 %psum.64 = f32[16]{0:T(128)S(1)} all-reduce(f32[16]{0:T(128)S(1)} %reduce_sum.426), channel_id=1, replica_groups=mesh['gx'=32,'gy'=8] {'gx','gy'}, use_global_device_ids=true, to_apply=%region_13.14 | all-reduce | flops 16 | bytes 128 | tf_op jit(solution)/shard_map/psum | solution.py:182
  266.3 4.4 select_reduce_fusion.11
  270.7 5.7 multiply_multiply_fusion.25
  276.4 8.8 scatter_custom_fusion.1
  288.8 3.3 collective-permute-done.9
  293.3 2.8 collective-permute-start.11
  305.6 8.4 gather_fusion.5
  314.6 84.7 %psum.65 = f32[16]{0:T(128)S(1)} all-reduce(f32[16]{0:T(128)S(1)} %reduce_sum.434), channel_id=1, replica_groups=mesh['gx'=32,'gy'=8] {'gx','gy'}, use_global_device_ids=true, to_apply=%region_20.21 | all-reduce | flops 16 | bytes 128 | tf_op jit(solution)/shard_map/psum | solution.py:182
  400.0 4.5 select_reduce_fusion.10
  404.6 5.7 multiply_multiply_fusion.24
  410.3 8.8 scatter_custom_fusion.2
  421.1 11.7 %gather_fusion.7 = f32[1536]{0:T(1024)} fusion(f32[2048]{0:T(1024)S(1)} %bitcast.826, s32[2048]{0:T(1024)S(1)} %copy-done.21), kind=kCustom, calls=%fused_computation.7 | custom fusion | bytes 18432 | tf_op jit(solution)/shard_map/gather | solution.py:234
  433.9 3.5 collective-permute-done.13
  439.3 3.3 collective-permute-start.15
  442.6 5.1 select_reduce_fusion.3
  455.5 8.4 gather_fusion.8
  465.3 81.7 %all-reduce.28 = (f32[16]{0:T(128)S(1)}, f32[16]{0:T(128)S(1)}) all-reduce(f32[16]{0:T(128)S(1)} %reduce_sum.455, f32[16]{0:T(128)S(1)} %reduce_sum.454), channel_id=1, replica_groups=mesh['gx'=32,'gy'=8] {'gx','gy'}, use_global_device_ids=true, to_apply=%region_34.35 | all-reduce | flops 32 | bytes 256 | tf_op jit(solution)/shard_map/psum | solution.py:182
  548.4 4.4 select_reduce_fusion.9
  552.9 4.5 select_reduce_fusion.8
  557.5 11.6 %fusion.186 = f32[1536]{0:T(1024)S(1)} fusion(pred[1536]{0:T(1024)(128)(4,1)S(1)} %copy-done.69, f32[1536]{0:T(1024)S(1)} %copy-done.5, pred[1536]{0:T(1024)(128)(4,1)S(1)} %copy-done.76, pred[1536]{0:T(1024)(128)(4,1)S(1)} %copy-done.84, pred[1536]{0:T(1024)(128)(4,1)S(1)} %copy-done.92, pred[1536]{0:T(1024)(128)(4,1)S(1)} %copy-done.100, ...), kind=kLoop, calls=%fused_computation.541 | loop fusion | flops 38400 | bytes 46152 | tf_op jit(solution)/shard_map/add | solution.py:240
  569.1 8.8 scatter_custom_fusion.3
  583.4 2.5 collective-permute-done.17
  586.1 3.9 collective-permute-start.19
  590.1 5.1 select_reduce_fusion.4
  597.0 2.2 reshape.1667
  600.7 8.4 gather_fusion.10
  609.6 80.4 %psum.68 = f32[16]{0:T(128)S(1)} all-reduce(f32[16]{0:T(128)S(1)} %reduce_sum.468), channel_id=1, replica_groups=mesh['gx'=32,'gy'=8] {'gx','gy'}, use_global_device_ids=true, to_apply=%region_42.43 | all-reduce | flops 16 | bytes 128 | tf_op jit(solution)/shard_map/psum | solution.py:182
  693.2 4.3 select_reduce_fusion.7
  697.6 11.3 fusion.184
  708.9 8.8 scatter_custom_fusion.4
  722.9 2.5 collective-permute-done.21
  725.6 3.7 collective-permute-start.23
  729.3 5.0 select_reduce_fusion.2
  736.2 2.2 reshape.1668
  739.8 8.4 gather_fusion.12
  748.6 80.9 %psum.69 = f32[16]{0:T(128)S(1)} all-reduce(f32[16]{0:T(128)S(1)} %reduce_sum.478), channel_id=1, replica_groups=mesh['gx'=32,'gy'=8] {'gx','gy'}, use_global_device_ids=true, to_apply=%region_50.51 | all-reduce | flops 16 | bytes 128 | tf_op jit(solution)/shard_map/psum | solution.py:182
  832.7 4.4 select_reduce_fusion.6
  837.3 11.3 fusion.182
  848.6 8.8 scatter_custom_fusion.5
  862.3 2.5 collective-permute-done.25
  865.0 3.8 collective-permute-start.27
  868.8 5.0 select_reduce_fusion.1
  879.3 8.4 gather_fusion.14
  888.2 81.0 %psum.70 = f32[16]{0:T(128)S(1)} all-reduce(f32[16]{0:T(128)S(1)} %reduce_sum.491), channel_id=1, replica_groups=mesh['gx'=32,'gy'=8] {'gx','gy'}, use_global_device_ids=true, to_apply=%region_58.59 | all-reduce | flops 16 | bytes 128 | tf_op jit(solution)/shard_map/psum | solution.py:182
  972.4 4.4 select_reduce_fusion.5
  977.0 11.2 fusion.180
  988.2 8.8 scatter_custom_fusion.6
  1000.9 4.5 select_reduce_fusion
  1005.9 3.4 collective-permute-start.31
  1009.5 50.7 %fusion.166 = f32[1536]{0:T(1024)S(1)} fusion(pred[1536]{0:T(1024)(128)(4,1)S(1)} %copy-done.72, pred[1536]{0:T(1024)(128)(4,1)S(1)} %copy-done.80, pred[1536]{0:T(1024)(128)(4,1)S(1)} %copy-done.88, pred[1536]{0:T(1024)(128)(4,1)S(1)} %copy-done.96, pred[1536]{0:T(1024)(128)(4,1)S(1)} %copy-done.104, pred[1536]{0:T(1024)(128)(4,1)S(1)} %copy-done.112, ...), kind=kLoop, calls=%fused_computation.513 | loop fusion | flops 190464 | bytes 126276 | tf_op jit(solution)/shard_map/add | solution.py:242
  1061.0 80.0 %psum.71 = f32[1536]{0:T(1024)} all-reduce(f32[1536]{0:T(1024)S(1)} %fusion.166), channel_id=1, replica_groups=mesh['gx'=32,'gy'=8] {'gx','gy'}, use_global_device_ids=true, to_apply=%region_60.61 | all-reduce | flops 1536 | bytes 12288 | tf_op jit(solution)/shard_map/psum | solution.py:247
  1142.8 2.2 reshape.1670
  (1152 shorter events, 106.0 us)
Async XLA Ops:
  2.0 14.3 %collective-permute-start = (f32[19,1,16,16]{3,2,1,0:T(8,128)S(1)}, f32[19,1,16,16]{3,2,1,0:T(8,128)S(1)}, u32[]{:S(2)}, u32[]{:S(2)}) collective-permute-start(f32[19,1,16,16]{3,2,1,0:T(8,128)S(1)} %get-tuple-element.69), channel_id=1, source_target_pairs={{0,8},{8,16},{16,24},{24,32},{32,40},{40,48},{48,56},{56,64},{64,7... | collective-permute-start | bytes 58376 | tf_op jit(solution)/shard_map/ppermute | solution.py:25
  4.7 11.8 %collective-permute-start.1 = (f32[19,1,16,16]{3,2,1,0:T(8,128)S(1)}, f32[19,1,16,16]{3,2,1,0:T(8,128)S(1)}, u32[]{:S(2)}, u32[]{:S(2)}) collective-permute-start(f32[19,1,16,16]{3,2,1,0:T(8,128)S(1)} %get-tuple-element.68), channel_id=1, source_target_pairs={{8,0},{16,8},{24,16},{32,24},{40,32},{48,40},{56,48},{64,56},{72,6... | collective-permute-start | bytes 58376 | tf_op jit(solution)/shard_map/ppermute | solution.py:26
  5.5 132.0 %copy-start.73 = (pred[1536]{0:T(1024)(128)(4,1)}, pred[1536]{0:T(1024)(128)(4,1)S(1)}, u32[]{:S(2)}) copy-start(pred[1536]{0:T(1024)(128)(4,1)S(1)} %compare_reduce_fusion) | copy-start | bytes 4612
  5.5 132.0 %copy-start.81 = (pred[1536]{0:T(1024)(128)(4,1)}, pred[1536]{0:T(1024)(128)(4,1)S(1)}, u32[]{:S(2)}) copy-start(pred[1536]{0:T(1024)(128)(4,1)S(1)} %compare_reduce_fusion.1) | copy-start | bytes 4612
  5.6 131.9 %copy-start.89 = (pred[1536]{0:T(1024)(128)(4,1)}, pred[1536]{0:T(1024)(128)(4,1)S(1)}, u32[]{:S(2)}) copy-start(pred[1536]{0:T(1024)(128)(4,1)S(1)} %compare_reduce_fusion.2) | copy-start | bytes 4612
  5.7 131.8 %copy-start.97 = (pred[1536]{0:T(1024)(128)(4,1)}, pred[1536]{0:T(1024)(128)(4,1)S(1)}, u32[]{:S(2)}) copy-start(pred[1536]{0:T(1024)(128)(4,1)S(1)} %compare_reduce_fusion.3) | copy-start | bytes 4612
  5.8 131.8 %copy-start.105 = (pred[1536]{0:T(1024)(128)(4,1)}, pred[1536]{0:T(1024)(128)(4,1)S(1)}, u32[]{:S(2)}) copy-start(pred[1536]{0:T(1024)(128)(4,1)S(1)} %compare_reduce_fusion.4) | copy-start | bytes 4612
  5.8 131.7 %copy-start.113 = (pred[1536]{0:T(1024)(128)(4,1)}, pred[1536]{0:T(1024)(128)(4,1)S(1)}, u32[]{:S(2)}) copy-start(pred[1536]{0:T(1024)(128)(4,1)S(1)} %compare_reduce_fusion.5) | copy-start | bytes 4612
  5.9 137.3 %copy-start.255 = (s32[1536]{0:T(1024)}, s32[1536]{0:T(1024)S(1)}, u32[]{:S(2)}) copy-start(s32[1536]{0:T(1024)S(1)} %compare_select_fusion.1) | copy-start | bytes 18436
  7.4 130.1 %copy-start.121 = (pred[1536]{0:T(1024)(128)(4,1)}, pred[1536]{0:T(1024)(128)(4,1)S(1)}, u32[]{:S(2)}) copy-start(pred[1536]{0:T(1024)(128)(4,1)S(1)} %compare_reduce_fusion.6) | copy-start | bytes 4612
  17.8 5.6 collective-permute-start.2
  18.5 5.0 collective-permute-start.3
  21.5 116.0 %copy-start.129 = (pred[1536]{0:T(1024)(128)(4,1)}, pred[1536]{0:T(1024)(128)(4,1)S(1)}, u32[]{:S(2)}) copy-start(pred[1536]{0:T(1024)(128)(4,1)S(1)} %compare_reduce_fusion.7) | copy-start | bytes 4612
  22.4 115.2 %copy-start.137 = (pred[1536]{0:T(1024)(128)(4,1)}, pred[1536]{0:T(1024)(128)(4,1)S(1)}, u32[]{:S(2)}) copy-start(pred[1536]{0:T(1024)(128)(4,1)S(1)} %compare_reduce_fusion.8) | copy-start | bytes 4612
  27.9 124.0 %copy-start.52 = (f32[1,2,8,128]{3,1,2,0:T(2,128)}, f32[1,2,8,128]{3,1,2,0:T(2,128)S(1)}, u32[]{:S(2)}) copy-start(f32[1,2,8,128]{3,1,2,0:T(2,128)S(1)} %copy.360) | copy-start | bytes 24580
  28.8 123.1 %copy-start.212 = (f32[2048]{0:T(1024)}, f32[2048]{0:T(1024)S(1)}, u32[]{:S(2)}) copy-start(f32[2048]{0:T(1024)S(1)} %broadcast_multiply_fusion.15) | copy-start | bytes 24580
  29.9 122.4 %copy-start.218 = (f32[2048]{0:T(1024)}, f32[2048]{0:T(1024)S(1)}, u32[]{:S(2)}) copy-start(f32[2048]{0:T(1024)S(1)} %get-tuple-element.23) | copy-start | bytes 24580
  29.9 122.0 %copy-start.59 = (f32[15,19]{1,0:T(8,128)S(1)}, f32[15,19]{1,0:T(8,128)}, u32[]{:S(2)}) copy-start(f32[15,19]{1,0:T(8,128)} %constant.153.clone) | copy-start | bytes 3424
  29.9 122.4 %copy-start.34 = (f32[19,6]{1,0:T(8,128)S(1)}, f32[19,6]{1,0:T(8,128)}, u32[]{:S(2)}) copy-start(f32[19,6]{1,0:T(8,128)} %constant.154.clone) | copy-start | bytes 1372
  29.9 122.7 %copy-start.40 = (f32[19,9]{1,0:T(8,128)S(1)}, f32[19,9]{1,0:T(8,128)}, u32[]{:S(2)}) copy-start(f32[19,9]{1,0:T(8,128)} %constant.155.clone) | copy-start | bytes 2056
  29.9 122.7 %copy-start.263 = (f32[19]{0:T(128)S(1)}, f32[19]{0:T(128)}, u32[]{:S(2)}) copy-start(f32[19]{0:T(128)} %constant.157.clone) | copy-start | bytes 232
  38.4 113.9 %copy-start.145 = (f32[1536]{0:T(1024)}, f32[1536]{0:T(1024)S(1)}, u32[]{:S(2)}) copy-start(f32[1536]{0:T(1024)S(1)} %gather_fusion.1) | copy-start | bytes 18436
  49.6 103.1 %copy-start.66 = (pred[1536]{0:T(1024)(128)(4,1)}, pred[1536]{0:T(1024)(128)(4,1)S(1)}, u32[]{:S(2)}) copy-start(pred[1536]{0:T(1024)(128)(4,1)S(1)} %get-tuple-element.37) | copy-start | bytes 4612
  153.5 2.6 collective-permute-start.4
  153.9 4.7 collective-permute-start.5
  158.8 6.6 collective-permute-start.6
  159.3 6.1 collective-permute-start.7
  172.1 113.1 %copy-start.220 = (f32[2048]{0:T(1024)}, f32[2048]{0:T(1024)S(1)}, u32[]{:S(2)}) copy-start(f32[2048]{0:T(1024)S(1)} %get-tuple-element.27) | copy-start | bytes 24580
  172.2 113.0 %copy-start.35 = (f32[19,6]{1,0:T(8,128)S(1)}, f32[19,6]{1,0:T(8,128)}, u32[]{:S(2)}) copy-start(f32[19,6]{1,0:T(8,128)} %constant.154.clone) | copy-start | bytes 1372
  172.2 113.3 %copy-start.41 = (f32[19,9]{1,0:T(8,128)S(1)}, f32[19,9]{1,0:T(8,128)}, u32[]{:S(2)}) copy-start(f32[19,9]{1,0:T(8,128)} %constant.155.clone) | copy-start | bytes 2056
  172.3 113.3 %copy-start.264 = (f32[19]{0:T(128)S(1)}, f32[19]{0:T(128)}, u32[]{:S(2)}) copy-start(f32[19]{0:T(128)} %constant.157.clone) | copy-start | bytes 232
  180.7 104.8 %copy-start.148 = (f32[1536]{0:T(1024)}, f32[1536]{0:T(1024)S(1)}, u32[]{:S(2)}) copy-start(f32[1536]{0:T(1024)S(1)} %gather_fusion.3) | copy-start | bytes 18436
  181.3 104.2 %copy-start.15 = (f32[15,2048]{1,0:T(8,128)}, f32[15,2048]{1,0:T(8,128)S(1)}, u32[]{:S(2)}) copy-start(f32[15,2048]{1,0:T(8,128)S(1)} %fusion.261) | copy-start | bytes 368644
  286.4 2.3 collective-permute-start.8
  287.4 4.7 collective-permute-start.9
  292.2 6.5 collective-permute-start.10
  293.3 5.4 collective-permute-start.11
  305.5 113.6 %copy-start.222 = (f32[2048]{0:T(1024)}, f32[2048]{0:T(1024)S(1)}, u32[]{:S(2)}) copy-start(f32[2048]{0:T(1024)S(1)} %get-tuple-element.31) | copy-start | bytes 24580
  305.6 113.5 %copy-start.36 = (f32[19,6]{1,0:T(8,128)S(1)}, f32[19,6]{1,0:T(8,128)}, u32[]{:S(2)}) copy-start(f32[19,6]{1,0:T(8,128)} %constant.154.clone) | copy-start | bytes 1372
  305.6 113.9 %copy-start.42 = (f32[19,9]{1,0:T(8,128)S(1)}, f32[19,9]{1,0:T(8,128)}, u32[]{:S(2)}) copy-start(f32[19,9]{1,0:T(8,128)} %constant.155.clone) | copy-start | bytes 2056
  305.6 113.9 %copy-start.266 = (f32[19]{0:T(128)S(1)}, f32[19]{0:T(128)}, u32[]{:S(2)}) copy-start(f32[19]{0:T(128)} %constant.157.clone) | copy-start | bytes 232
  314.1 105.4 %copy-start.151 = (f32[1536]{0:T(1024)}, f32[1536]{0:T(1024)S(1)}, u32[]{:S(2)}) copy-start(f32[1536]{0:T(1024)S(1)} %gather_fusion.5) | copy-start | bytes 18436
  314.6 104.8 %copy-start.17 = (f32[15,2048]{1,0:T(8,128)}, f32[15,2048]{1,0:T(8,128)S(1)}, u32[]{:S(2)}) copy-start(f32[15,2048]{1,0:T(8,128)S(1)} %fusion.257) | copy-start | bytes 368644
  420.3 13.6 %collective-permute-start.12 = (f32[19,1,16,16]{3,2,1,0:T(8,128)S(1)}, f32[19,1,16,16]{3,2,1,0:T(8,128)S(1)}, u32[]{:S(2)}, u32[]{:S(2)}) collective-permute-start(f32[19,1,16,16]{3,2,1,0:T(8,128)S(1)} %get-tuple-element.63), channel_id=1, source_target_pairs={{0,8},{8,16},{16,24},{24,32},{32,40},{40,48},{48,56},{56,64},{64,7... | collective-permute-start | bytes 58376 | tf_op jit(solution)/shard_map/ppermute | solution.py:25
  432.8 4.7 collective-permute-start.13
  438.8 10.4 collective-permute-start.14
  439.3 9.9 collective-permute-start.15
  463.9 114.8 %copy-start.232 = (f32[1536]{0:T(1024)}, f32[1536]{0:T(1024)S(1)}, u32[]{:S(2)}) copy-start(f32[1536]{0:T(1024)S(1)} %gather_fusion.8) | copy-start | bytes 18436
  579.7 3.6 collective-permute-start.16
  581.2 4.7 collective-permute-start.17
  586.0 9.1 collective-permute-start.18
  586.1 9.0 collective-permute-start.19
  719.5 3.4 collective-permute-start.20
  720.7 4.7 collective-permute-start.21
  725.5 8.8 collective-permute-start.22
  725.6 8.7 collective-permute-start.23
  859.2 3.1 collective-permute-start.24
  860.1 4.7 collective-permute-start.25
  865.0 8.9 collective-permute-start.26
  865.0 8.8 collective-permute-start.27
  999.1 6.4 collective-permute-start.28
  1000.1 5.3 collective-permute-start.29
  1005.7 135.3 %collective-permute-start.30 = (f32[19,10,1,16]{3,2,1,0:T(1,128)S(1)}, f32[19,10,1,16]{3,2,1,0:T(1,128)S(1)}, u32[]{:S(2)}, u32[]{:S(2)}) collective-permute-start(f32[19,10,1,16]{3,2,1,0:T(1,128)S(1)} %get-tuple-element.38), channel_id=1, source_target_pairs={{0,1},{1,2},{2,3},{3,4},{4,5},{5,6},{6,7},{7,0},{8,9},{9,10},{10,1... | collective-permute-start | bytes 36488 | tf_op jit(solution)/shard_map/ppermute | solution.py:25
  1005.9 135.1 %collective-permute-start.31 = (f32[19,10,1,16]{3,2,1,0:T(1,128)S(1)}, f32[19,10,1,16]{3,2,1,0:T(1,128)S(1)}, u32[]{:S(2)}, u32[]{:S(2)}) collective-permute-start(f32[19,10,1,16]{3,2,1,0:T(1,128)S(1)} %get-tuple-element.39), channel_id=1, source_target_pairs={{1,0},{2,1},{3,2},{4,3},{5,4},{6,5},{7,6},{0,7},{9,8},{10,9},{11,1... | collective-permute-start | bytes 36488 | tf_op jit(solution)/shard_map/ppermute | solution.py:26
  (243 other events, 7864.3 us)
where the time goes:
time: 1160 us; the launch traced here: 1150 us
  blocking collectives  655 us (56%)
  other arithmetic  277 us (24%)
  local copies, waits for them, and re-layouts  125 us (11%)
  starting transfers between devices  41.8 us (4%)
  waiting for transfers between devices  23 us (2%)
  matrix products  17.3 us (1%)
    psum x7, blocking collectives, turbine_total(): return lax.psum(partial_value, ('gx', 'gy'))  575 us
    psum x1, blocking collectives, body(): grad_area = lax.psum(area_grad, ('gx', 'gy'))  80 us
    add x1, other arithmetic, body(): area_grad + mine * rotor_bar[turbine] * (sampled - rotor_here) / denom[tu...  50.7 us
    add x4, other arithmetic, body(): sample_bar = sample_bar + numer_bar[turbine] * blade_area * mine  45.4 us
    gather x4, local copies, waits for them, and re-layouts, body(): thrust_bar = force_bar[point_local] * mine  36.9 us
    scatter-add x4, other arithmetic, body(): speed_bar = jnp.zeros((cells,), jnp.float32).at[point_local].add(sample_bar)  35.2 us
    gather x4, local copies, waits for them, and re-layouts, body(): sampled = velocity_local(flat)[point_local] * mine  33.6 us
    ppermute x16, starting transfers between devices, extended(): after = lax.ppermute(first, axis, down)  30.8 us
  transfers between devices with their start and end apart: 32, of which 14 were waited for; matrix products, arithmetic and copies ran while one was open for 10% of the time, Pallas kernels for 0%

commit v1 on v0

--- a/solution.py
+++ b/solution.py
@@ -244,7 +244,7 @@
         unused_speed, speed_pull = jax.vjp(velocity_local, flat)
         flat_bar = flat_bar + speed_pull(speed_bar)[0]
         adjoint = stream_adjoint(flat_bar.reshape(pops, width_x, span))
-    grad_area = lax.psum(area_grad, ("gx", "gy"))
+    grad_area = jnp.sum(lax.all_gather(area_grad, ("gx", "gy")), axis=0)
     return (adjoint, grad_area)
 
 

time: 1160 us -> 1780 us (1.53)
  waiting for transfers between devices: 23 us -> 701 us
  blocking collectives: 655 us -> 575 us
    all_gather x0 -> x1, waiting for transfers between devices: none -> 677 us  [body(): grad_area = jnp.sum(lax.all_gather(area_grad, ('gx', 'gy')), axis=0)]
    psum x1 -> x0, blocking collectives: 80 us -> none  [body(): grad_area = lax.psum(area_grad, ('gx', 'gy'))]
  transfers between devices with their start and end apart: 32 -> 33, of which waited for: 14 -> 16; matrix products, arithmetic and copies ran while one was open for 10% -> 7% of each run, Pallas kernels for 0% -> 0%
where the time goes in v1:
time: 1780 us; the launch traced here: 1760 us
  waiting for transfers between devices  701 us (39%)
  blocking collectives  575 us (32%)
  other arithmetic  280 us (16%)
  local copies, waits for them, and re-layouts  125 us (7%)
  starting transfers between devices  42.1 us (2%)
  between operations  21.3 us (1%)
    all_gather x1, waiting for transfers between devices, body(): grad_area = jnp.sum(lax.all_gather(area_grad, ('gx', 'gy')), axis=0)  677 us
    psum x7, blocking collectives, turbine_total(): return lax.psum(partial_value, ('gx', 'gy'))  575 us
    add x1, other arithmetic, body(): area_grad + mine * rotor_bar[turbine] * (sampled - rotor_here) / denom[tu...  50.8 us
    add x4, other arithmetic, body(): sample_bar = sample_bar + numer_bar[turbine] * blade_area * mine  45.4 us
    gather x4, local copies, waits for them, and re-layouts, body(): thrust_bar = force_bar[point_local] * mine  36.9 us
  transfers between devices with their start and end apart: 33, of which 16 were waited for; matrix products, arithmetic and copies ran while one was open for 7% of the time, Pallas kernels for 0%

profile of v1, /device:TPU:1, one launch (start us, length us, event | category | flops | bytes accessed | tf_op | source)
XLA Modules:
  0.0 1762.9 jit_solution(18349628436391774068)
XLA Ops:
  8.6 2.7 collective-permute-start
  14.0 8.9 select_reduce_fusion.13
  25.1 3.0 collective-permute-start.3
  36.6 8.4 gather_fusion.1
  45.0 11.2 fusion.199
  56.5 82.5 %psum.56 = f32[16]{0:T(128)S(1)} all-reduce(f32[16]{0:T(128)S(1)} %reduce_sum.422), channel_id=1, replica_groups=mesh['gx'=32,'gy'=8] {'gx','gy'}, use_global_device_ids=true, to_apply=%region_5.6 | all-reduce | flops 16 | bytes 128 | tf_op jit(solution)/shard_map/psum | solution.py:182
  139.7 4.4 select_reduce_fusion.12
  144.1 5.6 multiply_multiply_fusion.26
  149.8 8.7 scatter_custom_fusion
  162.7 2.4 collective-permute-done.5
  165.8 3.2 collective-permute-start.7
  178.8 8.4 gather_fusion.3
  187.8 84.2 %psum.57 = f32[16]{0:T(128)S(1)} all-reduce(f32[16]{0:T(128)S(1)} %reduce_sum.434), channel_id=1, replica_groups=mesh['gx'=32,'gy'=8] {'gx','gy'}, use_global_device_ids=true, to_apply=%region_13.14 | all-reduce | flops 16 | bytes 128 | tf_op jit(solution)/shard_map/psum | solution.py:182
  272.8 4.5 select_reduce_fusion.11
  277.4 5.8 multiply_multiply_fusion.25
  283.1 8.8 scatter_custom_fusion.1
  295.5 3.3 collective-permute-done.9
  300.0 2.8 collective-permute-start.11
  312.4 8.4 gather_fusion.5
  321.4 84.6 %psum.58 = f32[16]{0:T(128)S(1)} all-reduce(f32[16]{0:T(128)S(1)} %reduce_sum.442), channel_id=1, replica_groups=mesh['gx'=32,'gy'=8] {'gx','gy'}, use_global_device_ids=true, to_apply=%region_20.21 | all-reduce | flops 16 | bytes 128 | tf_op jit(solution)/shard_map/psum | solution.py:182
  406.8 4.3 select_reduce_fusion.10
  411.2 5.6 multiply_multiply_fusion.24
  416.8 8.8 scatter_custom_fusion.2
  427.5 11.7 gather_fusion.7
  440.4 3.5 collective-permute-done.13
  445.8 3.3 collective-permute-start.15
  449.1 4.9 select_reduce_fusion.3
  461.8 8.4 gather_fusion.8
  471.5 81.7 %all-reduce.28 = (f32[16]{0:T(128)S(1)}, f32[16]{0:T(128)S(1)}) all-reduce(f32[16]{0:T(128)S(1)} %reduce_sum.463, f32[16]{0:T(128)S(1)} %reduce_sum.462), channel_id=1, replica_groups=mesh['gx'=32,'gy'=8] {'gx','gy'}, use_global_device_ids=true, to_apply=%region_34.35 | all-reduce | flops 32 | bytes 256 | tf_op jit(solution)/shard_map/psum | solution.py:182
  554.7 4.4 select_reduce_fusion.9
  559.1 4.6 select_reduce_fusion.8
  563.8 11.5 fusion.186
  575.3 8.8 scatter_custom_fusion.3
  589.6 2.5 collective-permute-done.17
  592.3 3.9 collective-permute-start.19
  596.3 5.0 select_reduce_fusion.4
  606.9 8.4 gather_fusion.10
  615.7 80.4 %psum.61 = f32[16]{0:T(128)S(1)} all-reduce(f32[16]{0:T(128)S(1)} %reduce_sum.476), channel_id=1, replica_groups=mesh['gx'=32,'gy'=8] {'gx','gy'}, use_global_device_ids=true, to_apply=%region_42.43 | all-reduce | flops 16 | bytes 128 | tf_op jit(solution)/shard_map/psum | solution.py:182
  699.4 4.4 select_reduce_fusion.7
  703.9 11.1 fusion.184
  715.0 8.8 scatter_custom_fusion.4
  729.0 2.5 collective-permute-done.21
  731.7 3.7 collective-permute-start.23
  735.4 5.0 select_reduce_fusion.2
  742.3 2.2 reshape.1672
  745.9 8.4 gather_fusion.12
  754.8 80.9 %psum.62 = f32[16]{0:T(128)S(1)} all-reduce(f32[16]{0:T(128)S(1)} %reduce_sum.489), channel_id=1, replica_groups=mesh['gx'=32,'gy'=8] {'gx','gy'}, use_global_device_ids=true, to_apply=%region_50.51 | all-reduce | flops 16 | bytes 128 | tf_op jit(solution)/shard_map/psum | solution.py:182
  838.9 4.4 select_reduce_fusion.6
  843.4 11.4 fusion.182
  854.8 8.8 scatter_custom_fusion.5
  868.6 2.5 collective-permute-done.25
  871.4 3.8 collective-permute-start.27
  875.1 5.0 select_reduce_fusion.1
  882.0 2.2 reshape.1673
  885.7 8.4 gather_fusion.14
  894.5 81.0 %psum.63 = f32[16]{0:T(128)S(1)} all-reduce(f32[16]{0:T(128)S(1)} %reduce_sum.499), channel_id=1, replica_groups=mesh['gx'=32,'gy'=8] {'gx','gy'}, use_global_device_ids=true, to_apply=%region_58.59 | all-reduce | flops 16 | bytes 128 | tf_op jit(solution)/shard_map/psum | solution.py:182
  979.4 4.5 select_reduce_fusion.5
  984.0 11.4 fusion.180
  995.4 8.8 scatter_custom_fusion.6
  1007.3 4.5 select_reduce_fusion
  1012.1 50.8 %fusion.166 = f32[1536]{0:T(1024)S(1)} fusion(pred[1536]{0:T(1024)(128)(4,1)S(1)} %copy-done.72, pred[1536]{0:T(1024)(128)(4,1)S(1)} %copy-done.80, pred[1536]{0:T(1024)(128)(4,1)S(1)} %copy-done.88, pred[1536]{0:T(1024)(128)(4,1)S(1)} %copy-done.96, pred[1536]{0:T(1024)(128)(4,1)S(1)} %copy-done.104, pred[1536]{0:T(1024)(128)(4,1)S(1)} %copy-done.112, ...), kind=kLoop, calls=%fused_computation.513 | loop fusion | flops 190464 | bytes 126276 | tf_op jit(solution)/shard_map/add | solution.py:242
  1064.0 3.7 collective-permute-start.31
  1075.4 677.2 %all-gather.4.cloned.1.call-done = f32[256,1,1536]{2,1,0:T(1,128)} async-done(((f32[1,1,1536]{2,1,0:T(1,128)}), f32[256,1,1536]{2,1,0:T(1,128)}) %all-gather.4.cloned.1.call-update) | async-done | bytes 1572880 | tf_op jit(solution)/shard_map/all_gather | solution.py:247
  1752.7 2.9 reduce_sum.503
  (1152 shorter events, 109.9 us)
Async XLA Ops:
  7.2 1745.5 %all-gather.4.cloned.1.call-start = ((), (), s32[]{:S(2)}) async-start(), calls=%async_computation | async-start | bytes 1579008 | tf_op jit(solution)/shard_map/all_gather | solution.py:247
  8.6 14.4 collective-permute-start
  11.2 11.9 collective-permute-start.1
  12.0 132.0 %copy-start.73 = (pred[1536]{0:T(1024)(128)(4,1)}, pred[1536]{0:T(1024)(128)(4,1)S(1)}, u32[]{:S(2)}) copy-start(pred[1536]{0:T(1024)(128)(4,1)S(1)} %compare_reduce_fusion) | copy-start | bytes 4612
  12.1 132.0 %copy-start.81 = (pred[1536]{0:T(1024)(128)(4,1)}, pred[1536]{0:T(1024)(128)(4,1)S(1)}, u32[]{:S(2)}) copy-start(pred[1536]{0:T(1024)(128)(4,1)S(1)} %compare_reduce_fusion.1) | copy-start | bytes 4612
  12.2 131.9 %copy-start.89 = (pred[1536]{0:T(1024)(128)(4,1)}, pred[1536]{0:T(1024)(128)(4,1)S(1)}, u32[]{:S(2)}) copy-start(pred[1536]{0:T(1024)(128)(4,1)S(1)} %compare_reduce_fusion.2) | copy-start | bytes 4612
  12.2 131.8 %copy-start.97 = (pred[1536]{0:T(1024)(128)(4,1)}, pred[1536]{0:T(1024)(128)(4,1)S(1)}, u32[]{:S(2)}) copy-start(pred[1536]{0:T(1024)(128)(4,1)S(1)} %compare_reduce_fusion.3) | copy-start | bytes 4612
  12.3 131.8 %copy-start.105 = (pred[1536]{0:T(1024)(128)(4,1)}, pred[1536]{0:T(1024)(128)(4,1)S(1)}, u32[]{:S(2)}) copy-start(pred[1536]{0:T(1024)(128)(4,1)S(1)} %compare_reduce_fusion.4) | copy-start | bytes 4612
  12.4 131.7 %copy-start.113 = (pred[1536]{0:T(1024)(128)(4,1)}, pred[1536]{0:T(1024)(128)(4,1)S(1)}, u32[]{:S(2)}) copy-start(pred[1536]{0:T(1024)(128)(4,1)S(1)} %compare_reduce_fusion.5) | copy-start | bytes 4612
  12.5 137.3 %copy-start.253 = (s32[1536]{0:T(1024)}, s32[1536]{0:T(1024)S(1)}, u32[]{:S(2)}) copy-start(s32[1536]{0:T(1024)S(1)} %compare_select_fusion.1) | copy-start | bytes 18436
  14.0 130.1 %copy-start.121 = (pred[1536]{0:T(1024)(128)(4,1)}, pred[1536]{0:T(1024)(128)(4,1)S(1)}, u32[]{:S(2)}) copy-start(pred[1536]{0:T(1024)(128)(4,1)S(1)} %compare_reduce_fusion.6) | copy-start | bytes 4612
  24.4 5.6 collective-permute-start.2
  25.1 5.0 collective-permute-start.3
  28.1 116.0 %copy-start.129 = (pred[1536]{0:T(1024)(128)(4,1)}, pred[1536]{0:T(1024)(128)(4,1)S(1)}, u32[]{:S(2)}) copy-start(pred[1536]{0:T(1024)(128)(4,1)S(1)} %compare_reduce_fusion.7) | copy-start | bytes 4612
  29.0 115.1 %copy-start.137 = (pred[1536]{0:T(1024)(128)(4,1)}, pred[1536]{0:T(1024)(128)(4,1)S(1)}, u32[]{:S(2)}) copy-start(pred[1536]{0:T(1024)(128)(4,1)S(1)} %compare_reduce_fusion.8) | copy-start | bytes 4612
  34.5 124.0 %copy-start.52 = (f32[1,2,8,128]{3,1,2,0:T(2,128)}, f32[1,2,8,128]{3,1,2,0:T(2,128)S(1)}, u32[]{:S(2)}) copy-start(f32[1,2,8,128]{3,1,2,0:T(2,128)S(1)} %copy.512) | copy-start | bytes 24580
  35.4 123.0 %copy-start.210 = (f32[2048]{0:T(1024)}, f32[2048]{0:T(1024)S(1)}, u32[]{:S(2)}) copy-start(f32[2048]{0:T(1024)S(1)} %broadcast_multiply_fusion.15) | copy-start | bytes 24580
  36.5 122.3 %copy-start.216 = (f32[2048]{0:T(1024)}, f32[2048]{0:T(1024)S(1)}, u32[]{:S(2)}) copy-start(f32[2048]{0:T(1024)S(1)} %get-tuple-element.23) | copy-start | bytes 24580
  36.5 122.0 %copy-start.59 = (f32[15,19]{1,0:T(8,128)S(1)}, f32[15,19]{1,0:T(8,128)}, u32[]{:S(2)}) copy-start(f32[15,19]{1,0:T(8,128)} %constant.153.clone) | copy-start | bytes 3424
  36.5 122.3 %copy-start.34 = (f32[19,6]{1,0:T(8,128)S(1)}, f32[19,6]{1,0:T(8,128)}, u32[]{:S(2)}) copy-start(f32[19,6]{1,0:T(8,128)} %constant.154.clone) | copy-start | bytes 1372
  36.5 122.6 %copy-start.40 = (f32[19,9]{1,0:T(8,128)S(1)}, f32[19,9]{1,0:T(8,128)}, u32[]{:S(2)}) copy-start(f32[19,9]{1,0:T(8,128)} %constant.155.clone) | copy-start | bytes 2056
  36.5 122.6 %copy-start.261 = (f32[19]{0:T(128)S(1)}, f32[19]{0:T(128)}, u32[]{:S(2)}) copy-start(f32[19]{0:T(128)} %constant.157.clone) | copy-start | bytes 232
  45.0 113.8 %copy-start.145 = (f32[1536]{0:T(1024)}, f32[1536]{0:T(1024)S(1)}, u32[]{:S(2)}) copy-start(f32[1536]{0:T(1024)S(1)} %gather_fusion.1) | copy-start | bytes 18436
  160.0 2.6 collective-permute-start.4
  160.4 4.7 collective-permute-start.5
  165.3 6.6 collective-permute-start.6
  165.8 6.1 collective-permute-start.7
  178.6 113.3 %copy-start.218 = (f32[2048]{0:T(1024)}, f32[2048]{0:T(1024)S(1)}, u32[]{:S(2)}) copy-start(f32[2048]{0:T(1024)S(1)} %get-tuple-element.27) | copy-start | bytes 24580
  178.8 113.2 %copy-start.35 = (f32[19,6]{1,0:T(8,128)S(1)}, f32[19,6]{1,0:T(8,128)}, u32[]{:S(2)}) copy-start(f32[19,6]{1,0:T(8,128)} %constant.154.clone) | copy-start | bytes 1372
  178.8 113.5 %copy-start.41 = (f32[19,9]{1,0:T(8,128)S(1)}, f32[19,9]{1,0:T(8,128)}, u32[]{:S(2)}) copy-start(f32[19,9]{1,0:T(8,128)} %constant.155.clone) | copy-start | bytes 2056
  178.8 113.5 %copy-start.262 = (f32[19]{0:T(128)S(1)}, f32[19]{0:T(128)}, u32[]{:S(2)}) copy-start(f32[19]{0:T(128)} %constant.157.clone) | copy-start | bytes 232
  187.2 105.0 %copy-start.148 = (f32[1536]{0:T(1024)}, f32[1536]{0:T(1024)S(1)}, u32[]{:S(2)}) copy-start(f32[1536]{0:T(1024)S(1)} %gather_fusion.3) | copy-start | bytes 18436
  187.8 104.5 %copy-start.15 = (f32[15,2048]{1,0:T(8,128)}, f32[15,2048]{1,0:T(8,128)S(1)}, u32[]{:S(2)}) copy-start(f32[15,2048]{1,0:T(8,128)S(1)} %fusion.261) | copy-start | bytes 368644
  293.1 2.3 collective-permute-start.8
  294.2 4.7 collective-permute-start.9
  299.0 6.5 collective-permute-start.10
  300.0 5.4 collective-permute-start.11
  312.2 113.4 %copy-start.220 = (f32[2048]{0:T(1024)}, f32[2048]{0:T(1024)S(1)}, u32[]{:S(2)}) copy-start(f32[2048]{0:T(1024)S(1)} %get-tuple-element.31) | copy-start | bytes 24580
  312.3 113.3 %copy-start.36 = (f32[19,6]{1,0:T(8,128)S(1)}, f32[19,6]{1,0:T(8,128)}, u32[]{:S(2)}) copy-start(f32[19,6]{1,0:T(8,128)} %constant.154.clone) | copy-start | bytes 1372
  312.3 113.6 %copy-start.42 = (f32[19,9]{1,0:T(8,128)S(1)}, f32[19,9]{1,0:T(8,128)}, u32[]{:S(2)}) copy-start(f32[19,9]{1,0:T(8,128)} %constant.155.clone) | copy-start | bytes 2056
  312.3 113.6 %copy-start.264 = (f32[19]{0:T(128)S(1)}, f32[19]{0:T(128)}, u32[]{:S(2)}) copy-start(f32[19]{0:T(128)} %constant.157.clone) | copy-start | bytes 232
  320.8 105.1 %copy-start.151 = (f32[1536]{0:T(1024)}, f32[1536]{0:T(1024)S(1)}, u32[]{:S(2)}) copy-start(f32[1536]{0:T(1024)S(1)} %gather_fusion.5) | copy-start | bytes 18436
  321.4 104.5 %copy-start.17 = (f32[15,2048]{1,0:T(8,128)}, f32[15,2048]{1,0:T(8,128)S(1)}, u32[]{:S(2)}) copy-start(f32[15,2048]{1,0:T(8,128)S(1)} %fusion.257) | copy-start | bytes 368644
  426.7 13.6 collective-permute-start.12
  439.3 4.7 collective-permute-start.13
  445.2 10.2 collective-permute-start.14
  445.8 9.6 collective-permute-start.15
  470.2 114.8 %copy-start.230 = (f32[1536]{0:T(1024)}, f32[1536]{0:T(1024)S(1)}, u32[]{:S(2)}) copy-start(f32[1536]{0:T(1024)S(1)} %gather_fusion.8) | copy-start | bytes 18436
  586.0 3.6 collective-permute-start.16
  587.4 4.7 collective-permute-start.17
  592.2 9.1 collective-permute-start.18
  592.3 9.0 collective-permute-start.19
  725.7 3.3 collective-permute-start.20
  726.8 4.7 collective-permute-start.21
  731.6 8.8 collective-permute-start.22
  731.7 8.7 collective-permute-start.23
  865.4 3.2 collective-permute-start.24
  866.5 4.7 collective-permute-start.25
  871.3 8.9 collective-permute-start.26
  871.4 8.8 collective-permute-start.27
  1006.3 57.3 %collective-permute-start.28 = (f32[19,1,16,16]{3,2,1,0:T(8,128)S(1)}, f32[19,1,16,16]{3,2,1,0:T(8,128)S(1)}, u32[]{:S(2)}, u32[]{:S(2)}) collective-permute-start(f32[19,1,16,16]{3,2,1,0:T(8,128)S(1)} %get-tuple-element.54), channel_id=1, source_target_pairs={{0,8},{8,16},{16,24},{24,32},{32,40},{40,48},{48,56},{56,64},{64,7... | collective-permute-start | bytes 58376 | tf_op jit(solution)/shard_map/ppermute | solution.py:25
  1007.3 56.3 %collective-permute-start.29 = (f32[19,1,16,16]{3,2,1,0:T(8,128)S(1)}, f32[19,1,16,16]{3,2,1,0:T(8,128)S(1)}, u32[]{:S(2)}, u32[]{:S(2)}) collective-permute-start(f32[19,1,16,16]{3,2,1,0:T(8,128)S(1)} %get-tuple-element.55), channel_id=1, source_target_pairs={{8,0},{16,8},{24,16},{32,24},{40,32},{48,40},{56,48},{64,56},{72,6... | collective-permute-start | bytes 58376 | tf_op jit(solution)/shard_map/ppermute | solution.py:26
  1063.8 5.6 collective-permute-start.30
  1064.0 5.4 collective-permute-start.31
  (242 other events, 7945.3 us)
Sparse Core Ops, SparseCore 0:
  1063.6 689.0 all-gather.3
